TPU v7x, 32 devices: a whole 2x2x4 slice. The times are simulated.
32 devices in a mesh: site: 32 (over z, y, x, core).
Axes of the slice: x: 2, y: 2, z: 4, core: 2. Of those that a mesh axis runs over, the one named last changes fastest.
Arguments:
- sites: float32 [32, 2, 12, 128, 128], P('site'), may hold values from -0.5 to 0.5
- sector_sizes: int32 [32, 12], P('site'), may hold values from 64 to 128, as said below
- charge_steps: int32 [32], P('site'), may hold values from 0 to 1
- kept_counts: int32 [32, 12], P('site'), may hold values from 64 to 128, as said below
- gates: float32 [32, 6], P('site'), may hold values from 0.4 to 1.2
- sketches: float32 [32, 12, 256, 128], P('site'), may hold values from -0.375 to 0.375
Outputs:
- new_sites: float32 [32, 2, 12, 128, 128], P('site')
- totals: float32 [2], replicated
Inputs may be any that keep to these rules, and one draw needn't show every extreme that they name: `sector_sizes`: every sector holds at least 64 states; each bond has one sector of exactly 128 states. kept_counts[i, c] is at least 64 and at most sector_sizes[(i + 1) mod 32, c]; on each bond the sector of 128 states keeps all of them.
All inputs are finite; a program needn't handle non-finite values.
Results may differ from a plain program's by a relative error of at most 0.0003.
Values sent between devices are 32-bit elements; how exact they have to be, the bound alone decides.
A program may use at most 64 MiB of HBM per device.

v0:
```python
import functools

import jax
import jax.numpy as jnp
from jax import lax
from jax.experimental import pallas as pl
from jax.experimental.pallas import tpu as pltpu
from jax.sharding import PartitionSpec as P

STEPS = 4
HI = lax.Precision.HIGHEST


def mm(a, b, ca=1, cb=0):
    return lax.dot_general(
        a, b, (((ca,), (cb,)), ((), ())), precision=HI, preferred_element_type=jnp.float32
    )


def inverse_factors(w_ref, z_ref, n, width):
    strip = 32
    lanes = lax.broadcasted_iota(jnp.int32, (1, 8, width), 2)
    subs = lax.broadcasted_iota(jnp.int32, (1, 8, width), 1)
    for b in range(width // strip):
        r0 = b * strip
        groups = strip // 8
        ps = [w_ref[:, r0 + 8 * g : r0 + 8 * g + 8, :] for g in range(groups)]
        if b == 0:
            zs = [
                jnp.broadcast_to((lanes == subs + 8 * g).astype(jnp.float32), ps[0].shape)
                for g in range(groups)
            ]
        else:
            zs = [z_ref[:, r0 + 8 * g : r0 + 8 * g + 8, :] for g in range(groups)]
        for q in range(groups):
            vs = [
                [
                    jnp.broadcast_to(
                        ps[g][:, :, r0 + 8 * q + t : r0 + 8 * q + t + 1], ps[g].shape
                    )
                    if g >= q
                    else None
                    for g in range(groups)
                ]
                for t in range(8)
            ]
            for t in range(8):
                piv = vs[t][q][:, t : t + 1, :]
                inv = lax.rsqrt(piv)
                inv = inv * (1.5 - 0.5 * piv * inv * inv)
                inv2 = inv * inv

                def eliminate(rows):
                    pivot_row = rows[q][:, t : t + 1, :]
                    scaled = pivot_row * inv2
                    out = list(rows)
                    lower = rows[q] - vs[t][q] * scaled
                    out[q] = jnp.where(
                        subs > t, lower, jnp.where(subs == t, rows[q] * inv, rows[q])
                    )
                    for g in range(q + 1, groups):
                        out[g] = rows[g] - vs[t][g] * scaled
                    return out

                ps = eliminate(ps)
                zs = eliminate(zs)
                for t2 in range(t + 1, 8):
                    vs[t2] = eliminate(vs[t2])
        for g in range(groups):
            z_ref[:, r0 + 8 * g : r0 + 8 * g + 8, :] = zs[g]
            w_ref[:, r0 + 8 * g : r0 + 8 * g + 8, :] = ps[g]
        r1 = r0 + strip
        if r1 < width:
            rest = width - r1

            def trail(k, carry, r0=r0, r1=r1, rest=rest, b=b):
                pk = w_ref[k, r0:r1, :]
                zk = z_ref[k, r0:r1, :]
                both = mm(pk, jnp.concatenate([pk, zk], axis=1), 0, 0)[r1:]
                w_ref[k, r1:, :] = w_ref[k, r1:, :] - both[:, :width]
                if b == 0:
                    ri = lax.broadcasted_iota(jnp.int32, (rest, width), 0) + r1
                    ci = lax.broadcasted_iota(jnp.int32, (rest, width), 1)
                    old = (ri == ci).astype(jnp.float32)
                else:
                    old = z_ref[k, r1:, :]
                z_ref[k, r1:, :] = old - both[:, width:]
                return carry

            lax.fori_loop(0, n, trail, 0, unroll=True)


def sweep_kernel(
    n, width, sweep, kept, gate,
    own, trav, ex_o, ex_t, own_sk, got_sk,
    own_out, trav_out, ex2, ex3,
    xl, xr, mat, smp, w_ref, z_ref, tot, wgt,
):
    full = 2 * n * width
    me = lax.axis_index("site")
    chain = lax.axis_size("site")
    is_left = lax.rem(me, 2) == sweep
    idle = ((me == 0) | (me == chain - 1)) if sweep == 1 else (me < 0)
    which = jnp.where(is_left, 0, 1)

    prev_total = own[full : full + 1, :] + ex_o[2 * width : 2 * width + 1, :]
    prev_weight = own[full + 1 : full + 2, :] + ex_o[2 * width + 1 : 2 * width + 2, :]
    lost = own[full + 2 : full + 3, :] + (1.0 - prev_weight / prev_total)
    logs = own[full + 3 : full + 4, :] + jnp.log(prev_total)
    other_weight = trav[full + 1 : full + 2, :] + ex_t[2 * width + 1 : 2 * width + 2, :]
    scale = 1.0 / jnp.sqrt(jnp.where(is_left, prev_weight, other_weight))

    for p in range(2):
        er = pl.ds(p * width, width)
        eo = ex_o[er, :]
        et = ex_t[er, :]
        xl[p, 0] = jnp.where(is_left, eo, et) * scale
        xr[p, n] = jnp.where(is_left, et, eo)
        for k in range(n):
            hr = pl.ds((p * n + k) * width, width)
            ho = own[hr, :]
            ht = trav[hr, :]
            xl[p, k + 1] = jnp.where(is_left, ho, ht) * scale
            xr[p, k] = jnp.where(is_left, ht, ho)

    def put(k, p, left_block, right_block):
        hr = pl.ds(pl.multiple_of((p * n + k) * width, width), width)
        own_out[hr, :] = jnp.where(is_left, left_block, right_block)
        trav_out[hr, :] = jnp.where(is_left, right_block, left_block)

    def stats(total, weight):
        rows = lax.broadcasted_iota(jnp.int32, (8, width), 0)
        tile = jnp.where(rows == 0, total, jnp.where(rows == 1, weight, 0.0))
        tile = jnp.where(rows == 2, lost, jnp.where(rows == 3, logs, tile))
        own_out[full : full + 8, :] = tile
        trav_out[full : full + 8, :] = tile
        ex2[2 * width : 2 * width + 8, :] = tile
        ex3[2 * width : 2 * width + 8, :] = tile

    @pl.when(idle)
    def _():
        for k in range(n):
            put(k, 0, xl[0, k + 1], xr[0, k])
            put(k, 1, xl[1, k], xr[1, k + 1])
        half = jnp.full((8, width), 0.5, jnp.float32)
        stats(half, half)

    @pl.when(jnp.logical_not(idle))
    def _():
        g = [gate[which, i] for i in range(6)]

        def mixes(j, carry):
            s01 = mm(xl[0, j], xr[1, j])
            s10 = mm(xl[1, j], xr[0, j])

            @pl.when(j > 0)
            def _():
                mat[jnp.maximum(j - 1, 0), :width, width:] = g[2] * s01 + g[3] * s10

            @pl.when(j < n)
            def _():
                mat[jnp.minimum(j, n - 1), width:, :width] = g[4] * s01 + g[5] * s10

            return carry

        lax.fori_loop(0, n + 1, mixes, 0, unroll=True)
        tot[...] = jnp.zeros_like(tot)
        wgt[...] = jnp.zeros_like(wgt)
        eye = (
            lax.broadcasted_iota(jnp.int32, (width, width), 0)
            == lax.broadcasted_iota(jnp.int32, (width, width), 1)
        )
        cols = lax.broadcasted_iota(jnp.int32, (1, width), 1)

        def first(k, carry):
            mat[k, :width, :width] = g[0] * mm(xl[0, k + 1], xr[0, k])
            mat[k, width:, width:] = g[1] * mm(xl[1, k], xr[1, k + 1])
            m = mat[k]
            sq = jnp.sum(m * m, axis=0, keepdims=True)
            tot[0:1, :] += sq[:, :width] + sq[:, width:]
            used = cols < kept[which, k]
            s = mm(m, jnp.where(used, jnp.where(is_left, own_sk[k], got_sk[k]), 0.0))
            smp[k] = s
            gram = mm(s, s, 0, 0)
            ds = jnp.sum(jnp.sum(s * s, axis=0, keepdims=True), axis=1, keepdims=True)
            kf = kept[which, k].astype(jnp.float32)
            ridge = 0.001 * ds / kf + 1e-06
            add = ridge + jnp.where(used, 0.0, 1.0)
            w_ref[k] = gram + jnp.where(eye, add, 0.0)
            return carry

        lax.fori_loop(0, n, first, 0, unroll=2)
        inverse_factors(w_ref, z_ref, n, width)

        def second(k, carry):
            basis = mm(smp[k], z_ref[k], 1, 1)
            red = mm(basis, mat[k], 0, 0)
            sq = jnp.sum(red * red, axis=0, keepdims=True)
            wgt[0:1, :] += sq[:, :width] + sq[:, width:]
            put(k, 0, basis[:width], red[:, :width])
            put(k, 1, basis[width:], red[:, width:])
            return carry

        lax.fori_loop(0, n, second, 0, unroll=2)
        t = jnp.sum(tot[0:1, :], axis=1, keepdims=True)
        wt = jnp.sum(wgt[0:1, :], axis=1, keepdims=True)
        stats(jnp.broadcast_to(t, (8, width)), jnp.broadcast_to(wt, (8, width)))

    for p in range(2):
        er = pl.ds(p * width, width)
        low = pl.ds(p * n * width, width)
        high = pl.ds((p * n + n - 1) * width, width)
        ex2[er, :] = jnp.where(is_left, trav_out[high, :], trav_out[low, :])
        ex3[er, :] = jnp.where(is_left, own_out[low, :], own_out[high, :])


def run_sweep(n, width, sweep, kept, gate, own, trav, ex_o, ex_t, own_sk, got_sk):
    f32 = jnp.float32
    big = jax.ShapeDtypeStruct((2 * n * width + 8, width), f32)
    small = jax.ShapeDtypeStruct((2 * width + 8, width), f32)
    smem = pl.BlockSpec(memory_space=pltpu.SMEM)
    vmem = pl.BlockSpec(memory_space=pltpu.VMEM)
    return pl.pallas_call(
        functools.partial(sweep_kernel, n, width, sweep),
        out_shape=(big, big, small, small),
        in_specs=[smem] * 2 + [vmem] * 6,
        out_specs=(vmem,) * 4,
        scratch_shapes=[
            pltpu.VMEM((2, n + 1, width, width), f32),
            pltpu.VMEM((2, n + 1, width, width), f32),
            pltpu.VMEM((n, 2 * width, 2 * width), f32),
            pltpu.VMEM((n, 2 * width, width), f32),
            pltpu.VMEM((n, width, width), f32),
            pltpu.VMEM((n, width, width), f32),
            pltpu.VMEM((8, width), f32),
            pltpu.VMEM((8, width), f32),
        ],
        compiler_params=pltpu.CompilerParams(vmem_limit_bytes=40 * 1024 * 1024),
    )(kept, gate, own, trav, ex_o, ex_t, own_sk, got_sk)


MESH = pl.DeviceIdType.MESH


def even_partner(me, chain):
    return me + 1 - 2 * lax.rem(me, 2)


def odd_partner(me, chain):
    return lax.rem(me - 1 + 2 * lax.rem(me, 2) + chain, chain)


def ahead(by):
    return lambda me, chain: lax.rem(me + by + chain, chain)


def travel(sweep, back):
    def to(me, chain):
        by = 2 - 4 * lax.rem(me + sweep, 2)
        return lax.rem(me + (-by if back else by) + chain, chain)

    return to


def exchange_kernel(routes, *refs):
    me, chain = lax.axis_index("site"), lax.axis_size("site")
    count = len(routes)
    ins, outs, (send, recv) = refs[:count], refs[count : 2 * count], refs[2 * count :]
    barrier = pltpu.get_barrier_semaphore()
    for _, source in routes:
        pl.semaphore_signal(
            barrier, inc=1, device_id=(source(me, chain),), device_id_type=MESH
        )
    pl.semaphore_wait(barrier, count)
    copies = []
    for i, (to, _) in enumerate(routes):
        copy = pltpu.make_async_remote_copy(
            src_ref=ins[i], dst_ref=outs[i], send_sem=send.at[i], recv_sem=recv.at[i],
            device_id=(to(me, chain),), device_id_type=MESH,
        )
        copy.start()
        copies.append(copy)
    for copy in copies:
        copy.wait()


def exchange(cid, routes, *values):
    anywhere = pl.BlockSpec(memory_space=pl.ANY)
    count = len(routes)
    return pl.pallas_call(
        functools.partial(exchange_kernel, routes),
        out_shape=tuple(jax.ShapeDtypeStruct(v.shape, v.dtype) for v in values),
        in_specs=[anywhere] * count,
        out_specs=(anywhere,) * count,
        scratch_shapes=[pltpu.SemaphoreType.DMA((count,)), pltpu.SemaphoreType.DMA((count,))],
        compiler_params=pltpu.CompilerParams(collective_id=cid, has_side_effects=True),
    )(*values)


def spread_kernel(chain, routed, *refs):
    if routed:
        tile, value, out, value_out, send, recv, one_send, one_recv = refs
    else:
        tile, out, send, recv = refs
    me = lax.axis_index("site")
    barrier = pltpu.get_barrier_semaphore()

    def greet(off, carry):
        pl.semaphore_signal(
            barrier, inc=1, device_id=(lax.rem(me + off, chain),), device_id_type=MESH
        )
        return carry

    lax.fori_loop(1, chain, greet, 0)
    pl.semaphore_wait(barrier, chain - 1)
    if routed:
        one = pltpu.make_async_remote_copy(
            src_ref=value, dst_ref=value_out, send_sem=one_send, recv_sem=one_recv,
            device_id=(odd_partner(me, chain),), device_id_type=MESH,
        )
        one.start()

    def copy(off):
        return pltpu.make_async_remote_copy(
            src_ref=tile, dst_ref=out.at[me], send_sem=send.at[off], recv_sem=recv.at[off],
            device_id=(lax.rem(me + off, chain),), device_id_type=MESH,
        )

    def begin(off, carry):
        copy(off).start()
        return carry

    def finish(off, carry):
        copy(off).wait()
        return carry

    lax.fori_loop(1, chain, begin, 0)
    out[me] = tile[...]
    lax.fori_loop(1, chain, finish, 0)
    if routed:
        one.wait()


def spread(cid, chain, tile, value=None):
    vmem = pl.BlockSpec(memory_space=pltpu.VMEM)
    anywhere = pl.BlockSpec(memory_space=pl.ANY)
    routed = value is not None
    shapes = [jax.ShapeDtypeStruct((chain,) + tile.shape, tile.dtype)]
    sems = [pltpu.SemaphoreType.DMA((chain,)), pltpu.SemaphoreType.DMA((chain,))]
    ins, specs, args = [vmem], [vmem], [tile]
    if routed:
        shapes.append(jax.ShapeDtypeStruct(value.shape, value.dtype))
        sems += [pltpu.SemaphoreType.DMA, pltpu.SemaphoreType.DMA]
        ins, specs, args = [vmem, anywhere], [vmem, anywhere], [tile, value]
    return pl.pallas_call(
        functools.partial(spread_kernel, chain, routed),
        out_shape=tuple(shapes),
        in_specs=ins,
        out_specs=tuple(specs),
        scratch_shapes=sems,
        compiler_params=pltpu.CompilerParams(collective_id=cid, has_side_effects=True),
    )(*args)


def body(sites, sector_sizes, charge_steps, kept_counts, gates, sketches):
    f32 = jnp.float32
    chain = lax.axis_size("site")
    pos = lax.axis_index("site")
    count, width = sites.shape[2], sites.shape[-1]
    n = count // 2
    par = pos % 2
    odd = par == 1

    table = jnp.concatenate(
        [
            sector_sizes.astype(f32),
            kept_counts.astype(f32),
            charge_steps.astype(f32)[:, None],
            gates,
        ],
        axis=1,
    )
    used = table.shape[1]
    tile = jnp.pad(table, ((0, 7), (0, width - used)))
    table = spread(1, chain, tile)[0][:, 0, :used]
    steps = table[:, 2 * count].astype(jnp.int32)
    before = jnp.sum(jnp.where(jnp.arange(chain) < pos, steps, 0))
    step = charge_steps[0]
    prev = (pos + chain - 1) % chain
    following = lax.dynamic_index_in_dim(table, (pos + 1) % chain, 0, keepdims=False)[:count]
    prev_row = lax.dynamic_index_in_dim(table, prev, 0, keepdims=False)

    secs = jnp.arange(count, dtype=jnp.int32)
    mine = (secs[:n] + par * n)
    theirs = (secs[:n] + (1 - par) * n)
    order = jnp.concatenate(
        [
            mine,
            jnp.where(odd, 0, count - 1)[None].astype(jnp.int32),
            theirs,
            jnp.where(odd, n, n - 1)[None].astype(jnp.int32),
        ]
    )
    states = jnp.arange(width, dtype=jnp.int32)
    rows = states[None, :] < sector_sizes[0][:, None]
    pieces = []
    for p in range(2):
        label = (order - before - jnp.where(odd, p, 0)) % count
        target = (label + p - step) % count
        kr = rows[label]
        kc = states[None, :].astype(f32) < following[target][:, None]
        mask = kr[:, :, None] & kc[:, None, :]
        pieces.append(jnp.where(mask, sites[0, p][label], 0.0))
    both = jnp.stack(pieces)
    stat = jnp.where((jnp.arange(8) < 2)[:, None], 0.5, 0.0) * jnp.ones((1, width), f32)

    def flat(blocks):
        return jnp.concatenate([blocks.reshape(-1, width), stat], axis=0)

    own = flat(both[:, :n])
    ex_o = flat(both[:, n])
    after = before + step
    own_sk = sketches[0][(mine - after) % count]
    send_sk = sketches[0][(theirs - after) % count]
    trav, ex_t, got_sk = exchange(
        2,
        ((even_partner, even_partner), (even_partner, even_partner), (ahead(1), ahead(-1))),
        flat(both[:, n + 1 : 2 * n + 1]),
        flat(both[:, 2 * n + 1]),
        send_sk,
    )
    own_kept = kept_counts[0][(mine - after) % count]
    prev_kept = prev_row[count : 2 * count].astype(jnp.int32)[(mine - before) % count]
    kept = jnp.stack([own_kept, prev_kept])
    gate = jnp.stack([gates[0], prev_row[2 * count + 1 : used]])
    partners = (even_partner, odd_partner)

    def call(sweep, own, trav, ex_o, ex_t):
        return run_sweep(n, width, sweep, kept, gate, own, trav, ex_o, ex_t, own_sk, got_sk)

    def one_sweep(sweep, carry):
        own, trav, ex2, ex3 = call(sweep, *carry)
        near, far = partners[sweep], partners[1 - sweep]
        routes = ((travel(sweep, False), travel(sweep, True)), (near, near), (far, far))
        return (own,) + tuple(exchange(3 + sweep, routes, trav, ex2, ex3))

    carry = one_sweep(0, (own, trav, ex_o, ex_t))

    def pair(index, carry):
        return one_sweep(0, one_sweep(1, carry))

    carry = lax.fori_loop(0, STEPS - 1, pair, carry)
    own, trav, _, _ = call(1, *carry)
    full = 2 * n * width
    tiles, got = spread(5, chain, own[full:], trav)
    weight = own[full + 1, 0] + got[full + 1, 0]
    stats = tiles[:, :4, 0]
    bonds = jnp.sum(jnp.roll(stats[:, :2], -1, axis=0).reshape(chain // 2, 2, 2), axis=1)
    sums = jnp.stack(
        [
            0.5 * jnp.sum(stats[:, 2]) + jnp.sum(1.0 - bonds[:, 1] / bonds[:, 0]),
            0.5 * jnp.sum(stats[:, 3]) + jnp.sum(jnp.log(bonds[:, 0])),
        ]
    )
    scale = jnp.where(odd, 1.0, 1.0 / jnp.sqrt(weight))
    halves = jnp.stack(
        [own[:full].reshape(2, n, width, width), got[:full].reshape(2, n, width, width)], axis=1
    ).reshape(2, count, width, width)
    out = []
    for p in range(2):
        charge = (secs + before + jnp.where(odd, p, 0)) % count
        out.append(halves[p][(charge + par * n) % count])
    return ((jnp.stack(out) * scale)[None], sums)


def solution(mesh):
    placed = (
        P("site", None, None, None, None),
        P("site", None),
        P("site"),
        P("site", None),
        P("site", None),
        P("site", None, None, None),
    )
    return jax.shard_map(
        body,
        mesh=mesh,
        in_specs=placed,
        out_specs=(P("site", None, None, None, None), P()),
        check_vma=False,
    )
```

profile of v0, /device:TPU:0, one launch (start us, length us, event | category | flops | bytes accessed | tf_op | source)
XLA Modules:
  0.0 482.3 jit_solution(10240552946344289608)
XLA Ops:
  4.1 11.9 %shard_map.77 = f32[32,8,128]{2,1,0:T(8,128)} custom-call(f32[8,128]{1,0:T(8,128)} %select_maximum_fusion.refs_0_), custom_call_target="tpu_custom_call" | custom-call | tf_op jit(solution)/shard_map/pallas_call | solution.py:355
  21.5 1.5 gather_fusion.7
  26.7 1.5 gather_fusion.4
  32.2 1.5 gather_fusion.8
  33.7 15.8 %shard_map.78 = (f32[1544,128]{1,0:T(8,128)}, f32[264,128]{1,0:T(8,128)}, f32[6,256,128]{2,1,0:T(8,128)}) custom-call(f32[1544,128]{1,0:T(8,128)} %get-tuple-element.135.refs_0_, f32[264,128]{1,0:T(8,128)} %get-tuple-element.134.refs_1_, f32[6,256,128]{2,1,0:T(8,128)} %gather_fusion.8), custom_call_target="tpu_custom_call" | custom-call | tf_op jit(solution)/shard_map/pallas_call | solution.py:290
  49.5 1.5 gather_fusion.9
  52.4 39.0 %shard_map.79 = (f32[1544,128]{1,0:T(8,128)}, f32[1544,128]{1,0:T(8,128)S(1)}, f32[264,128]{1,0:T(8,128)S(1)}, f32[264,128]{1,0:T(8,128)S(1)}) custom-call(s32[2,6]{1,0:T(2,128)S(1)} %pad_add_fusion.kept, f32[2,6]{1,0:T(2,128)S(1)} %pad_maximum_fusion.6.gate, f32[1544,128]{1,0:T(8,128)S(1)} %get-tuple-element.136.own, f32[1544,128]{1,0:T(8,128)S(1)} %copy-done.11, ...), custom_call_target="tpu_custom_call" | custom-call | tf_op jit(solution)/shard_map/pallas_call | solution.py:223
  93.6 19.9 %shard_map.80 = (f32[1544,128]{1,0:T(8,128)}, f32[264,128]{1,0:T(8,128)S(1)}, f32[264,128]{1,0:T(8,128)S(1)}) custom-call(f32[1544,128]{1,0:T(8,128)} %copy-done.12, f32[264,128]{1,0:T(8,128)} %copy-done.14, f32[264,128]{1,0:T(8,128)} %copy-done.15), custom_call_target="tpu_custom_call" | custom-call | tf_op jit(solution)/shard_map/pallas_call | solution.py:290
  113.6 299.3 %while.16 = (s32[]{:T(128)}, f32[1544,128]{1,0:T(8,128)}, f32[1544,128]{1,0:T(8,128)}, f32[264,128]{1,0:T(8,128)S(1)}, f32[264,128]{1,0:T(8,128)S(1)}, /*index=5...) while((s32[]{:T(128)}, f32[1544,128]{1,0:T(8,128)}, ...), condition=%wide.region_2.3_spmd, body=%wide.region_1.2_spmd.sunk | while | flops 2 | bytes 15876477 | solution.py:452
  113.6 2.2 eval_jaxpr.4
  118.0 40.2 %eval_jaxpr.5 = (f32[1544,128]{1,0:T(8,128)}, f32[264,128]{1,0:T(8,128)}, f32[264,128]{1,0:T(8,128)}) custom-call(f32[1544,128]{1,0:T(8,128)} %copy-done.2, f32[264,128]{1,0:T(8,128)} %copy-done.6, f32[264,128]{1,0:T(8,128)} %copy-done.7), custom_call_target="tpu_custom_call" | custom-call | tf_op jit(solution)/shard_map/while/body/eval_jaxpr/pallas_call | solution.py:290
  161.1 21.3 %eval_jaxpr.6 = (f32[1544,128]{1,0:T(8,128)}, f32[1544,128]{1,0:T(8,128)S(1)}, f32[264,128]{1,0:T(8,128)S(1)}, f32[264,128]{1,0:T(8,128)S(1)}) custom-call(s32[2,6]{1,0:T(2,128)S(1)} %get-tuple-element.261.kept, f32[2,6]{1,0:T(2,128)S(1)} %get-tuple-element.262.gate, f32[1544,128]{1,0:T(8,128)S(1)} %get-tuple-element.222.own, f32[1544,128]{1,0:T(8,128)S(1)} %copy-done.1, ...), custom_call_target="tpu_custom_call" | custom-call | tf_op jit(solution)/shard_map/while/body/eval_jaxpr/pallas_call | solution.py:223
  184.7 25.3 %eval_jaxpr.7 = (f32[1544,128]{1,0:T(8,128)}, f32[264,128]{1,0:T(8,128)S(1)}, f32[264,128]{1,0:T(8,128)S(1)}) custom-call(f32[1544,128]{1,0:T(8,128)} %copy-done.3, f32[264,128]{1,0:T(8,128)} %copy-done.8, f32[264,128]{1,0:T(8,128)} %copy-done.9), custom_call_target="tpu_custom_call" | custom-call | tf_op jit(solution)/shard_map/while/body/eval_jaxpr/pallas_call | solution.py:290
  210.0 2.2 eval_jaxpr.4
  214.4 41.4 %eval_jaxpr.5 = (f32[1544,128]{1,0:T(8,128)}, f32[264,128]{1,0:T(8,128)}, f32[264,128]{1,0:T(8,128)}) custom-call(f32[1544,128]{1,0:T(8,128)} %copy-done.2, f32[264,128]{1,0:T(8,128)} %copy-done.6, f32[264,128]{1,0:T(8,128)} %copy-done.7), custom_call_target="tpu_custom_call" | custom-call | tf_op jit(solution)/shard_map/while/body/eval_jaxpr/pallas_call | solution.py:290
  258.8 21.3 %eval_jaxpr.6 = (f32[1544,128]{1,0:T(8,128)}, f32[1544,128]{1,0:T(8,128)S(1)}, f32[264,128]{1,0:T(8,128)S(1)}, f32[264,128]{1,0:T(8,128)S(1)}) custom-call(s32[2,6]{1,0:T(2,128)S(1)} %get-tuple-element.261.kept, f32[2,6]{1,0:T(2,128)S(1)} %get-tuple-element.262.gate, f32[1544,128]{1,0:T(8,128)S(1)} %get-tuple-element.222.own, f32[1544,128]{1,0:T(8,128)S(1)} %copy-done.1, ...), custom_call_target="tpu_custom_call" | custom-call | tf_op jit(solution)/shard_map/while/body/eval_jaxpr/pallas_call | solution.py:223
  282.3 24.0 %eval_jaxpr.7 = (f32[1544,128]{1,0:T(8,128)}, f32[264,128]{1,0:T(8,128)S(1)}, f32[264,128]{1,0:T(8,128)S(1)}) custom-call(f32[1544,128]{1,0:T(8,128)} %copy-done.3, f32[264,128]{1,0:T(8,128)} %copy-done.8, f32[264,128]{1,0:T(8,128)} %copy-done.9), custom_call_target="tpu_custom_call" | custom-call | tf_op jit(solution)/shard_map/while/body/eval_jaxpr/pallas_call | solution.py:290
  306.4 2.2 eval_jaxpr.4
  310.8 42.2 %eval_jaxpr.5 = (f32[1544,128]{1,0:T(8,128)}, f32[264,128]{1,0:T(8,128)}, f32[264,128]{1,0:T(8,128)}) custom-call(f32[1544,128]{1,0:T(8,128)} %copy-done.2, f32[264,128]{1,0:T(8,128)} %copy-done.6, f32[264,128]{1,0:T(8,128)} %copy-done.7), custom_call_target="tpu_custom_call" | custom-call | tf_op jit(solution)/shard_map/while/body/eval_jaxpr/pallas_call | solution.py:290
  356.0 21.3 %eval_jaxpr.6 = (f32[1544,128]{1,0:T(8,128)}, f32[1544,128]{1,0:T(8,128)S(1)}, f32[264,128]{1,0:T(8,128)S(1)}, f32[264,128]{1,0:T(8,128)S(1)}) custom-call(s32[2,6]{1,0:T(2,128)S(1)} %get-tuple-element.261.kept, f32[2,6]{1,0:T(2,128)S(1)} %get-tuple-element.262.gate, f32[1544,128]{1,0:T(8,128)S(1)} %get-tuple-element.222.own, f32[1544,128]{1,0:T(8,128)S(1)} %copy-done.1, ...), custom_call_target="tpu_custom_call" | custom-call | tf_op jit(solution)/shard_map/while/body/eval_jaxpr/pallas_call | solution.py:223
  379.5 23.8 %eval_jaxpr.7 = (f32[1544,128]{1,0:T(8,128)}, f32[264,128]{1,0:T(8,128)S(1)}, f32[264,128]{1,0:T(8,128)S(1)}) custom-call(f32[1544,128]{1,0:T(8,128)} %copy-done.3, f32[264,128]{1,0:T(8,128)} %copy-done.8, f32[264,128]{1,0:T(8,128)} %copy-done.9), custom_call_target="tpu_custom_call" | custom-call | tf_op jit(solution)/shard_map/while/body/eval_jaxpr/pallas_call | solution.py:290
  412.8 2.9 shard_map.81
  417.2 48.6 %shard_map.82 = (f32[32,8,128]{2,1,0:T(8,128)}, f32[1544,128]{1,0:T(8,128)}) custom-call(f32[8,128]{1,0:T(8,128)} %slice.108.refs_0_, f32[1544,128]{1,0:T(8,128)} %copy-done.10), custom_call_target="tpu_custom_call" | custom-call | tf_op jit(solution)/shard_map/pallas_call | solution.py:355
  479.7 2.4 maximum_multiply_fusion
  (142 shorter events, 52.1 us)
Async XLA Ops:
  0.6 31.5 %copy-start = (f32[1,12,256,128]{3,2,1,0:T(8,128)S(1)}, f32[1,12,256,128]{3,2,1,0:T(8,128)}, u32[]{:S(2)}) copy-start(f32[1,12,256,128]{3,2,1,0:T(8,128)} %param.13) | copy-start | bytes 4718596
  21.5 3.0 copy-start.20
  33.7 18.0 %copy-start.16 = (s32[1,12]{1,0:T(1,128)S(1)}, s32[1,12]{1,0:T(1,128)}, u32[]{:S(2)}) copy-start(s32[1,12]{1,0:T(1,128)} %param.11) | copy-start | bytes 148
  49.5 2.9 copy-start.19
  49.5 2.9 copy-start.11
  49.5 2.9 copy-start.13
  91.4 0.9 copy-start.12
  113.6 44.6 %copy-start.17 = (f32[6,256,128]{2,1,0:T(8,128)S(1)}, f32[6,256,128]{2,1,0:T(8,128)}, u32[]{:S(2)}) copy-start(f32[6,256,128]{2,1,0:T(8,128)} %get-tuple-element.263.own_sk) | copy-start | bytes 2359300 | tf_op jit(solution)/shard_map/while
  115.8 0.9 copy-start.2
  158.2 1.1 copy-start.1
  159.3 0.9 copy-start.4
  160.2 0.9 copy-start.5
  182.5 0.9 copy-start.3
  210.0 45.8 %copy-start.17 = (f32[6,256,128]{2,1,0:T(8,128)S(1)}, f32[6,256,128]{2,1,0:T(8,128)}, u32[]{:S(2)}) copy-start(f32[6,256,128]{2,1,0:T(8,128)} %get-tuple-element.263.own_sk) | copy-start | bytes 2359300 | tf_op jit(solution)/shard_map/while
  255.8 1.1 copy-start.1
  257.0 0.9 copy-start.4
  257.9 0.9 copy-start.5
  280.1 0.9 copy-start.3
  306.4 46.6 %copy-start.17 = (f32[6,256,128]{2,1,0:T(8,128)S(1)}, f32[6,256,128]{2,1,0:T(8,128)}, u32[]{:S(2)}) copy-start(f32[6,256,128]{2,1,0:T(8,128)} %get-tuple-element.263.own_sk) | copy-start | bytes 2359300 | tf_op jit(solution)/shard_map/while
  353.0 1.1 copy-start.1
  354.1 0.9 copy-start.4
  355.0 0.9 copy-start.5
  377.3 0.9 copy-start.3
  478.2 1.5 copy-start.18
  (17 other events, 11.7 us)
where the time goes:
time: 486 us; the launch traced here: 482 us
  Pallas kernels  406 us (84%)
  local copies, waits for them, and re-layouts  45.2 us (9%)
  other arithmetic  15.4 us (3%)
  loops' own time  9.78 us (2%)
  between operations  6.36 us (1%)
    pallas_call x8, Pallas kernels, exchange(): pl.pallas_call(functools.partial(exchange_kernel, routes), out_shape=tupl...  233 us
    pallas_call x8, Pallas kernels, run_sweep(): pl.pallas_call(functools.partial(sweep_kernel, n, width, sweep), out_shap...  112 us
    pallas_call x2, Pallas kernels, spread(): pl.pallas_call(functools.partial(spread_kernel, chain, routed), out_shape...  60.5 us
    while x60, local copies, waits for them, and re-layouts  22 us
    another operation x1, loops' own time, body(): carry = lax.fori_loop(0, STEPS - 1, pair, carry)  9.78 us

commit v1 on v0

--- a/solution.py
+++ b/solution.py
@@ -91,7 +91,7 @@
 
 
 def sweep_kernel(
-    n, width, sweep, kept, gate,
+    n, width, sweep, unroll, kept, gate,
     own, trav, ex_o, ex_t, own_sk, got_sk,
     own_out, trav_out, ex2, ex3,
     xl, xr, mat, smp, w_ref, z_ref, tot, wgt,
@@ -163,7 +163,7 @@
 
             return carry
 
-        lax.fori_loop(0, n + 1, mixes, 0, unroll=True)
+        lax.fori_loop(0, n + 1, mixes, 0, unroll=n + 1 if unroll > 1 else 1)
         tot[...] = jnp.zeros_like(tot)
         wgt[...] = jnp.zeros_like(wgt)
         eye = (
@@ -189,7 +189,7 @@
             w_ref[k] = gram + jnp.where(eye, add, 0.0)
             return carry
 
-        lax.fori_loop(0, n, first, 0, unroll=2)
+        lax.fori_loop(0, n, first, 0, unroll=unroll)
         inverse_factors(w_ref, z_ref, n, width)
 
         def second(k, carry):
@@ -201,7 +201,7 @@
             put(k, 1, basis[width:], red[:, width:])
             return carry
 
-        lax.fori_loop(0, n, second, 0, unroll=2)
+        lax.fori_loop(0, n, second, 0, unroll=unroll)
         t = jnp.sum(tot[0:1, :], axis=1, keepdims=True)
         wt = jnp.sum(wgt[0:1, :], axis=1, keepdims=True)
         stats(jnp.broadcast_to(t, (8, width)), jnp.broadcast_to(wt, (8, width)))
@@ -214,14 +214,14 @@
         ex3[er, :] = jnp.where(is_left, own_out[low, :], own_out[high, :])
 
 
-def run_sweep(n, width, sweep, kept, gate, own, trav, ex_o, ex_t, own_sk, got_sk):
+def run_sweep(n, width, sweep, unroll, kept, gate, own, trav, ex_o, ex_t, own_sk, got_sk):
     f32 = jnp.float32
     big = jax.ShapeDtypeStruct((2 * n * width + 8, width), f32)
     small = jax.ShapeDtypeStruct((2 * width + 8, width), f32)
     smem = pl.BlockSpec(memory_space=pltpu.SMEM)
     vmem = pl.BlockSpec(memory_space=pltpu.VMEM)
     return pl.pallas_call(
-        functools.partial(sweep_kernel, n, width, sweep),
+        functools.partial(sweep_kernel, n, width, sweep, unroll),
         out_shape=(big, big, small, small),
         in_specs=[smem] * 2 + [vmem] * 6,
         out_specs=(vmem,) * 4,
@@ -435,22 +435,22 @@
     gate = jnp.stack([gates[0], prev_row[2 * count + 1 : used]])
     partners = (even_partner, odd_partner)
 
-    def call(sweep, own, trav, ex_o, ex_t):
-        return run_sweep(n, width, sweep, kept, gate, own, trav, ex_o, ex_t, own_sk, got_sk)
-
-    def one_sweep(sweep, carry):
-        own, trav, ex2, ex3 = call(sweep, *carry)
+    def call(sweep, unroll, own, trav, ex_o, ex_t):
+        return run_sweep(n, width, sweep, unroll, kept, gate, own, trav, ex_o, ex_t, own_sk, got_sk)
+
+    def one_sweep(sweep, unroll, carry):
+        own, trav, ex2, ex3 = call(sweep, unroll, *carry)
         near, far = partners[sweep], partners[1 - sweep]
         routes = ((travel(sweep, False), travel(sweep, True)), (near, near), (far, far))
         return (own,) + tuple(exchange(3 + sweep, routes, trav, ex2, ex3))
 
-    carry = one_sweep(0, (own, trav, ex_o, ex_t))
+    carry = one_sweep(0, 1, (own, trav, ex_o, ex_t))
 
     def pair(index, carry):
-        return one_sweep(0, one_sweep(1, carry))
+        return one_sweep(0, 2, one_sweep(1, 2, carry))
 
     carry = lax.fori_loop(0, STEPS - 1, pair, carry)
-    own, trav, _, _ = call(1, *carry)
+    own, trav, _, _ = call(1, 1, *carry)
     full = 2 * n * width
     tiles, got = spread(5, chain, own[full:], trav)
     weight = own[full + 1, 0] + got[full + 1, 0]

time: 486 us -> 490 us (level)
  loops' own time: 9.78 us -> 25.6 us
  Pallas kernels: 406 us -> 394 us
    another operation x1, loops' own time: 9.78 us -> 25.6 us  [body(): carry = lax.fori_loop(0, STEPS - 1, pair, carry)]
    pallas_call x8, Pallas kernels: 112 us -> 98.2 us  [run_sweep(): pl.pallas_call(functools.partial(sweep_kernel, n, width, sweep, unroll),...]
where the time goes in v1:
time: 490 us; the launch traced here: 487 us
  Pallas kernels  394 us (80%)
  local copies, waits for them, and re-layouts  45.2 us (9%)
  loops' own time  25.6 us (5%)
  other arithmetic  15.4 us (3%)
  between operations  6.36 us (1%)
    pallas_call x8, Pallas kernels, exchange(): pl.pallas_call(functools.partial(exchange_kernel, routes), out_shape=tupl...  233 us
    pallas_call x8, Pallas kernels, run_sweep(): pl.pallas_call(functools.partial(sweep_kernel, n, width, sweep, unroll),...  98.2 us
    pallas_call x2, Pallas kernels, spread(): pl.pallas_call(functools.partial(spread_kernel, chain, routed), out_shape...  63.2 us
    another operation x1, loops' own time, body(): carry = lax.fori_loop(0, STEPS - 1, pair, carry)  25.6 us
    while x60, local copies, waits for them, and re-layouts  22 us

profile of v1, /device:TPU:0, one launch (start us, length us, event | category | flops | bytes accessed | tf_op | source)
XLA Modules:
  0.0 486.5 jit_solution(1908485978577124694)
XLA Ops:
  4.1 11.9 %shard_map.77 = f32[32,8,128]{2,1,0:T(8,128)} custom-call(f32[8,128]{1,0:T(8,128)} %select_maximum_fusion.refs_0_), custom_call_target="tpu_custom_call" | custom-call | tf_op jit(solution)/shard_map/pallas_call | solution.py:355
  21.5 1.5 gather_fusion.7
  26.7 1.5 gather_fusion.4
  32.2 1.5 gather_fusion.8
  33.7 15.8 %shard_map.78 = (f32[1544,128]{1,0:T(8,128)}, f32[264,128]{1,0:T(8,128)}, f32[6,256,128]{2,1,0:T(8,128)}) custom-call(f32[1544,128]{1,0:T(8,128)} %get-tuple-element.135.refs_0_, f32[264,128]{1,0:T(8,128)} %get-tuple-element.134.refs_1_, f32[6,256,128]{2,1,0:T(8,128)} %gather_fusion.8), custom_call_target="tpu_custom_call" | custom-call | tf_op jit(solution)/shard_map/pallas_call | solution.py:290
  49.5 1.5 gather_fusion.9
  52.4 24.7 %shard_map.79 = (f32[1544,128]{1,0:T(8,128)}, f32[1544,128]{1,0:T(8,128)S(1)}, f32[264,128]{1,0:T(8,128)S(1)}, f32[264,128]{1,0:T(8,128)S(1)}) custom-call(s32[2,6]{1,0:T(2,128)S(1)} %pad_add_fusion.kept, f32[2,6]{1,0:T(2,128)S(1)} %pad_maximum_fusion.6.gate, f32[1544,128]{1,0:T(8,128)S(1)} %get-tuple-element.136.own, f32[1544,128]{1,0:T(8,128)S(1)} %copy-done.11, ...), custom_call_target="tpu_custom_call" | custom-call | tf_op jit(solution)/shard_map/pallas_call | solution.py:223
  79.3 19.9 %shard_map.80 = (f32[1544,128]{1,0:T(8,128)}, f32[264,128]{1,0:T(8,128)S(1)}, f32[264,128]{1,0:T(8,128)S(1)}) custom-call(f32[1544,128]{1,0:T(8,128)} %copy-done.12, f32[264,128]{1,0:T(8,128)} %copy-done.14, f32[264,128]{1,0:T(8,128)} %copy-done.15), custom_call_target="tpu_custom_call" | custom-call | tf_op jit(solution)/shard_map/pallas_call | solution.py:290
  99.3 315.1 %while.16 = (s32[]{:T(128)}, f32[1544,128]{1,0:T(8,128)}, f32[1544,128]{1,0:T(8,128)}, f32[264,128]{1,0:T(8,128)S(1)}, f32[264,128]{1,0:T(8,128)S(1)}, /*index=5...) while((s32[]{:T(128)}, f32[1544,128]{1,0:T(8,128)}, ...), condition=%wide.region_2.3_spmd, body=%wide.region_1.2_spmd.sunk | while | flops 2 | bytes 15876477 | solution.py:452
  116.3 2.2 eval_jaxpr.4
  120.7 40.2 %eval_jaxpr.5 = (f32[1544,128]{1,0:T(8,128)}, f32[264,128]{1,0:T(8,128)}, f32[264,128]{1,0:T(8,128)}) custom-call(f32[1544,128]{1,0:T(8,128)} %copy-done.2, f32[264,128]{1,0:T(8,128)} %copy-done.6, f32[264,128]{1,0:T(8,128)} %copy-done.7), custom_call_target="tpu_custom_call" | custom-call | tf_op jit(solution)/shard_map/while/body/eval_jaxpr/pallas_call | solution.py:290
  163.8 21.3 %eval_jaxpr.6 = (f32[1544,128]{1,0:T(8,128)}, f32[1544,128]{1,0:T(8,128)S(1)}, f32[264,128]{1,0:T(8,128)S(1)}, f32[264,128]{1,0:T(8,128)S(1)}) custom-call(s32[2,6]{1,0:T(2,128)S(1)} %get-tuple-element.261.kept, f32[2,6]{1,0:T(2,128)S(1)} %get-tuple-element.262.gate, f32[1544,128]{1,0:T(8,128)S(1)} %get-tuple-element.222.own, f32[1544,128]{1,0:T(8,128)S(1)} %copy-done.1, ...), custom_call_target="tpu_custom_call" | custom-call | tf_op jit(solution)/shard_map/while/body/eval_jaxpr/pallas_call | solution.py:223
  187.4 25.3 %eval_jaxpr.7 = (f32[1544,128]{1,0:T(8,128)}, f32[264,128]{1,0:T(8,128)S(1)}, f32[264,128]{1,0:T(8,128)S(1)}) custom-call(f32[1544,128]{1,0:T(8,128)} %copy-done.3, f32[264,128]{1,0:T(8,128)} %copy-done.8, f32[264,128]{1,0:T(8,128)} %copy-done.9), custom_call_target="tpu_custom_call" | custom-call | tf_op jit(solution)/shard_map/while/body/eval_jaxpr/pallas_call | solution.py:290
  212.7 2.2 eval_jaxpr.4
  217.1 41.4 %eval_jaxpr.5 = (f32[1544,128]{1,0:T(8,128)}, f32[264,128]{1,0:T(8,128)}, f32[264,128]{1,0:T(8,128)}) custom-call(f32[1544,128]{1,0:T(8,128)} %copy-done.2, f32[264,128]{1,0:T(8,128)} %copy-done.6, f32[264,128]{1,0:T(8,128)} %copy-done.7), custom_call_target="tpu_custom_call" | custom-call | tf_op jit(solution)/shard_map/while/body/eval_jaxpr/pallas_call | solution.py:290
  261.5 21.3 %eval_jaxpr.6 = (f32[1544,128]{1,0:T(8,128)}, f32[1544,128]{1,0:T(8,128)S(1)}, f32[264,128]{1,0:T(8,128)S(1)}, f32[264,128]{1,0:T(8,128)S(1)}) custom-call(s32[2,6]{1,0:T(2,128)S(1)} %get-tuple-element.261.kept, f32[2,6]{1,0:T(2,128)S(1)} %get-tuple-element.262.gate, f32[1544,128]{1,0:T(8,128)S(1)} %get-tuple-element.222.own, f32[1544,128]{1,0:T(8,128)S(1)} %copy-done.1, ...), custom_call_target="tpu_custom_call" | custom-call | tf_op jit(solution)/shard_map/while/body/eval_jaxpr/pallas_call | solution.py:223
  285.0 24.0 %eval_jaxpr.7 = (f32[1544,128]{1,0:T(8,128)}, f32[264,128]{1,0:T(8,128)S(1)}, f32[264,128]{1,0:T(8,128)S(1)}) custom-call(f32[1544,128]{1,0:T(8,128)} %copy-done.3, f32[264,128]{1,0:T(8,128)} %copy-done.8, f32[264,128]{1,0:T(8,128)} %copy-done.9), custom_call_target="tpu_custom_call" | custom-call | tf_op jit(solution)/shard_map/while/body/eval_jaxpr/pallas_call | solution.py:290
  309.1 2.2 eval_jaxpr.4
  313.5 42.2 %eval_jaxpr.5 = (f32[1544,128]{1,0:T(8,128)}, f32[264,128]{1,0:T(8,128)}, f32[264,128]{1,0:T(8,128)}) custom-call(f32[1544,128]{1,0:T(8,128)} %copy-done.2, f32[264,128]{1,0:T(8,128)} %copy-done.6, f32[264,128]{1,0:T(8,128)} %copy-done.7), custom_call_target="tpu_custom_call" | custom-call | tf_op jit(solution)/shard_map/while/body/eval_jaxpr/pallas_call | solution.py:290
  358.6 21.3 %eval_jaxpr.6 = (f32[1544,128]{1,0:T(8,128)}, f32[1544,128]{1,0:T(8,128)S(1)}, f32[264,128]{1,0:T(8,128)S(1)}, f32[264,128]{1,0:T(8,128)S(1)}) custom-call(s32[2,6]{1,0:T(2,128)S(1)} %get-tuple-element.261.kept, f32[2,6]{1,0:T(2,128)S(1)} %get-tuple-element.262.gate, f32[1544,128]{1,0:T(8,128)S(1)} %get-tuple-element.222.own, f32[1544,128]{1,0:T(8,128)S(1)} %copy-done.1, ...), custom_call_target="tpu_custom_call" | custom-call | tf_op jit(solution)/shard_map/while/body/eval_jaxpr/pallas_call | solution.py:223
  382.2 23.8 %eval_jaxpr.7 = (f32[1544,128]{1,0:T(8,128)}, f32[264,128]{1,0:T(8,128)S(1)}, f32[264,128]{1,0:T(8,128)S(1)}) custom-call(f32[1544,128]{1,0:T(8,128)} %copy-done.3, f32[264,128]{1,0:T(8,128)} %copy-done.8, f32[264,128]{1,0:T(8,128)} %copy-done.9), custom_call_target="tpu_custom_call" | custom-call | tf_op jit(solution)/shard_map/while/body/eval_jaxpr/pallas_call | solution.py:290
  414.4 2.9 shard_map.81
  418.7 51.3 %shard_map.82 = (f32[32,8,128]{2,1,0:T(8,128)}, f32[1544,128]{1,0:T(8,128)}) custom-call(f32[8,128]{1,0:T(8,128)} %slice.108.refs_0_, f32[1544,128]{1,0:T(8,128)} %copy-done.10), custom_call_target="tpu_custom_call" | custom-call | tf_op jit(solution)/shard_map/pallas_call | solution.py:355
  483.9 2.4 maximum_multiply_fusion
  (142 shorter events, 52.1 us)
Async XLA Ops:
  0.6 31.5 %copy-start = (f32[1,12,256,128]{3,2,1,0:T(8,128)S(1)}, f32[1,12,256,128]{3,2,1,0:T(8,128)}, u32[]{:S(2)}) copy-start(f32[1,12,256,128]{3,2,1,0:T(8,128)} %param.13) | copy-start | bytes 4718596
  21.5 3.0 copy-start.20
  33.7 18.0 %copy-start.16 = (s32[1,12]{1,0:T(1,128)S(1)}, s32[1,12]{1,0:T(1,128)}, u32[]{:S(2)}) copy-start(s32[1,12]{1,0:T(1,128)} %param.11) | copy-start | bytes 148
  49.5 2.9 copy-start.19
  49.5 2.9 copy-start.11
  49.5 2.9 copy-start.13
  77.1 0.9 copy-start.12
  116.3 44.6 %copy-start.17 = (f32[6,256,128]{2,1,0:T(8,128)S(1)}, f32[6,256,128]{2,1,0:T(8,128)}, u32[]{:S(2)}) copy-start(f32[6,256,128]{2,1,0:T(8,128)} %get-tuple-element.263.own_sk) | copy-start | bytes 2359300 | tf_op jit(solution)/shard_map/while
  160.8 1.1 copy-start.1
  162.0 0.9 copy-start.4
  162.9 0.9 copy-start.5
  185.1 0.9 copy-start.3
  212.6 45.8 %copy-start.17 = (f32[6,256,128]{2,1,0:T(8,128)S(1)}, f32[6,256,128]{2,1,0:T(8,128)}, u32[]{:S(2)}) copy-start(f32[6,256,128]{2,1,0:T(8,128)} %get-tuple-element.263.own_sk) | copy-start | bytes 2359300 | tf_op jit(solution)/shard_map/while
  258.5 1.1 copy-start.1
  259.6 0.9 copy-start.4
  260.5 0.9 copy-start.5
  282.8 0.9 copy-start.3
  309.0 46.6 %copy-start.17 = (f32[6,256,128]{2,1,0:T(8,128)S(1)}, f32[6,256,128]{2,1,0:T(8,128)}, u32[]{:S(2)}) copy-start(f32[6,256,128]{2,1,0:T(8,128)} %get-tuple-element.263.own_sk) | copy-start | bytes 2359300 | tf_op jit(solution)/shard_map/while
  311.3 0.9 copy-start.2
  355.7 1.1 copy-start.1
  356.8 0.9 copy-start.4
  357.7 0.9 copy-start.5
  380.0 0.9 copy-start.3
  482.4 1.5 copy-start.18
  (17 other events, 11.7 us)
